TPU v7x, 128 devices: a whole 4x4x4 slice. The times are simulated.
128 devices in a mesh: dp: 16 (over y, z), mp: 8 (over x, core).
Axes of the slice: x: 4, y: 4, z: 4, core: 2. Of those that a mesh axis runs over, the one named last changes fastest.
Arguments:
- activations: bfloat16 [4, 8192, 5120], P(None, 'dp'), may hold values from -60 to 60
- task_weights: bfloat16 [4, 5120, 1024], P(None, 'dp', 'mp'), may hold values from -6 to 6
Outputs:
- merged: float32 [5120, 1024], P('dp', 'mp')
All inputs are finite; a program needn't handle non-finite values.
Results may differ from a plain program's by a relative error of at most 0.0015.
Values may be sent and summed in bfloat16 or wider, within the bound.
No kernel may reach another device: no remote copies, remote signals or barrier semaphores. Data moves between devices by JAX's collectives and lax.ppermute only.
A program may use at most 128 MiB of HBM per device.

v0:
```python
import jax
import jax.numpy as jnp
from jax import lax
from jax.sharding import PartitionSpec as P

ITERS = 2


ALPHA = 0.9


def column_sum(left, right):
    return jnp.sum(left * right, axis=0)


def shards(activations, task_weights):
    tasks, tokens, width = activations.shape
    n_rows = lax.axis_size("dp")
    n_cols = lax.axis_size("mp")
    block = width // n_cols
    rows_own = width // n_rows
    total = tasks * tokens * n_rows
    full_weights = lax.all_gather(task_weights, "dp", axis=1, tiled=True)
    outputs = jnp.einsum(
        "tnk,tkc->tnc", activations, full_weights, preferred_element_type=jnp.float32
    ).astype(jnp.bfloat16)
    squares = jnp.einsum(
        "tnk,tnk->tk", activations, activations, preferred_element_type=jnp.float32
    )
    own_cols = lax.dynamic_slice_in_dim(activations, lax.axis_index("mp") * block, block, 2)
    rows_x = activations
    gram_part = (
        jnp.einsum("tnk,tnc->kc", rows_x, own_cols, preferred_element_type=jnp.float32) / total
    )
    rows_x = activations
    cross = jnp.einsum("tnk,tnc->kc", rows_x, outputs, preferred_element_type=jnp.float32)
    w_rows = full_weights.astype(jnp.float32)
    diag_part = jnp.sum(squares[:, :, None] * w_rows, axis=0)
    terms = lax.psum_scatter(
        jnp.concatenate([gram_part, (ALPHA * cross + (1.0 - ALPHA) * diag_part) / total], axis=1),
        "dp",
        scatter_dimension=0,
        tiled=True,
    )
    gram_block = terms[:, :block]
    target = terms[:, block:]
    gram_rows = lax.all_gather(gram_block, "mp", axis=1, tiled=True)
    row_ids = lax.axis_index("dp") * rows_own + lax.broadcasted_iota(
        jnp.int32, (rows_own, width), 0
    )
    col_ids = lax.broadcasted_iota(jnp.int32, (rows_own, width), 1)
    operator = jnp.where(row_ids == col_ids, gram_rows, ALPHA * gram_rows)

    def apply(vector):
        return jnp.dot(
            operator,
            lax.all_gather(vector, "dp", axis=0, tiled=True),
            precision=lax.Precision.HIGHEST,
        )

    def norm_of(residual):
        return lax.psum(column_sum(residual, residual), "dp")

    merged = jnp.mean(task_weights.astype(jnp.float32), axis=0)
    residual = target - apply(merged)
    direction = residual
    norm_now = norm_of(residual)
    for step in range(ITERS):
        image = apply(direction)
        alpha = norm_now / lax.psum(column_sum(direction, image), "dp")
        merged = merged + alpha * direction
        if step + 1 < ITERS:
            residual = residual - alpha * image
            norm_next = norm_of(residual)
            direction = residual + norm_next / norm_now * direction
            norm_now = norm_next
    return merged


def solution(mesh):
    return jax.shard_map(
        shards,
        mesh=mesh,
        in_specs=(P(None, "dp", None), P(None, "dp", "mp")),
        out_specs=P("dp", "mp"),
        check_vma=False,
    )
```

profile of v0, /device:TPU:0, one launch (start us, length us, event | category | flops | bytes accessed | tf_op | source)
XLA Modules:
  0.0 592.5 jit_solution(14250781737191068932)
XLA Ops:
  6.5 0.0 all-gather.6.cloned.1.call-start
  6.5 0.7 all-gather.6.cloned.1.call-update
  7.3 0.0 reduce-scatter.4.cloned.1.call-start
  7.3 8.8 %fusion = f32[4,5120]{1,0:T(4,128)S(1)} fusion(bf16[4,512,5120]{2,1,0:T(8,128)(2,1)} %param.2), kind=kLoop, calls=%fused_computation.1 | loop fusion | flops 31436800 | bytes 21053440 | tf_op jit(solution)/shard_map/tnk,tnk->tk/dot_general | solution.py:27
  16.1 21.6 %fusion.1 = f32[5120,640]{0,1:T(8,128)} fusion(bf16[4,512,5120]{2,1,0:T(8,128)(2,1)} %param.2, s32[]{:T(128)S(6)} %select_n.7), kind=kOutput, calls=%fused_computation.4 | convolution fusion | flops 13425049600 | bytes 36700164 | tf_op jit(solution)/shard_map/tnk,tnc->kc/dot_general | solution.py:33
  37.7 30.8 %all-gather.6.cloned.1.call-done = bf16[4,5120,128]{2,1,0:T(8,128)(2,1)} async-done(((bf16[4,320,128]{2,1,0:T(8,128)(2,1)}), bf16[4,5120,128]{2,1,0:T(8,128)(2,1)}) %all-gather.6.cloned.1.call-update) | async-done | bytes 5242896 | tf_op jit(solution)/shard_map/all_gather | solution.py:23
  68.5 10.6 %multiply_reduce_fusion = f32[5120,128]{1,0:T(8,128)} fusion(bf16[4,5120,128]{2,1,0:T(8,128)(2,1)} %all-gather.6.cloned.1.call-done, f32[4,5120]{1,0:T(4,128)S(1)} %fusion), kind=kLoop, calls=%fused_computation.6 | loop fusion | flops 7208960 | bytes 7946240 | tf_op jit(solution)/shard_map/reduce_sum | solution.py:38
  79.1 2.1 copy.10
  81.2 24.6 %fusion.5 = f32[5120,128]{0,1:T(8,128)} fusion(bf16[4,512,5120]{2,1,0:T(8,128)(2,1)} %param.2, f32[5120,128]{0,1:T(8,128)S(1)} %copy.10, bf16[4,5120,128]{2,1,0:T(8,128)(2,1)} %all-gather.6.cloned.1.call-done), kind=kOutput, calls=%fused_computation.12 | convolution fusion | flops 5371592704 | bytes 31457280 | tf_op jit(solution)/shard_map/tnk,tnc->kc/dot_general | solution.py:36
  105.9 11.0 %pad_maximum_fusion = f32[5120,768]{0,1:T(8,128)} fusion(f32[5120,128]{0,1:T(8,128)} %fusion.5, f32[5120,640]{0,1:T(8,128)} %fusion.1), kind=kLoop, calls=%fused_computation.2 | loop fusion | flops 3932160 | bytes 31457280 | tf_op jit(solution)/shard_map/concatenate | solution.py:40
  116.8 15.7 %copy.18 = f32[5120,768]{1,0:T(8,128)} copy(f32[5120,768]{0,1:T(8,128)} %pad_maximum_fusion) | data formatting | bytes 31457280
  132.5 0.0 copy-start.2
  132.5 0.0 reduce-scatter.4.cloned.1.call-update
  132.6 0.0 all-gather.10.cloned.1.call-start
  132.6 0.9 copy-done.2
  133.6 0.7 broadcast_multiply_fusion
  134.2 0.0 all-gather.10.cloned.1.call-update
  134.3 0.2 all-gather.8.cloned.1.call-start
  134.5 103.6 %reduce-scatter.4.cloned.1.call-done = f32[320,768]{1,0:T(8,128)} async-done(((f32[5120,768]{1,0:T(8,128)}), f32[320,768]{1,0:T(8,128)}) %reduce-scatter.4.cloned.1.call-update) | async-done | bytes 983056 | tf_op jit(solution)/shard_map/reduce_scatter | solution.py:39
  238.1 1.2 slice.9
  239.3 1.3 copy.21
  240.6 0.0 all-gather.8.cloned.1.call-update
  240.6 0.0 all-gather.12.cloned.1.call-start
  240.6 45.3 %all-gather.10.cloned.1.call-done = f32[5120,128]{1,0:T(8,128)} async-done(((f32[320,128]{1,0:T(8,128)}), f32[5120,128]{1,0:T(8,128)}) %all-gather.10.cloned.1.call-update) | async-done | bytes 2621456 | tf_op jit(solution)/shard_map/all_gather | solution.py:57
  286.0 48.4 %all-gather.8.cloned.1.call-done = f32[320,5120]{0,1:T(8,128)} async-done(((f32[320,640]{0,1:T(8,128)}), f32[320,5120]{0,1:T(8,128)}) %all-gather.8.cloned.1.call-update) | async-done | bytes 6553616 | tf_op jit(solution)/shard_map/all_gather | solution.py:47
  334.3 16.0 %fusion.16 = f32[320,128]{1,0:T(8,128)} fusion(f32[5120,128]{1,0:T(8,128)} %all-gather.10.cloned.1.call-done, f32[320,5120]{0,1:T(8,128)} %all-gather.8.cloned.1.call-done, s32[320]{0:T(512)S(1)} %iota_add_fusion, f32[320,768]{1,0:T(8,128)} %reduce-scatter.4.cloned.1.call-done), kind=kOutput, calls=%fused_computation.24 | convolution fusion | flops 2521538560 | bytes 9504000 | tf_op jit(solution)/shard_map/dot_general | solution.py:55
  350.3 0.0 copy-start
  350.3 0.0 all-gather.12.cloned.1.call-update
  350.3 0.3 all-gather.14.cloned.1.call-start
  350.6 46.5 %all-gather.12.cloned.1.call-done = f32[5120,128]{1,0:T(8,128)} async-done(((f32[320,128]{1,0:T(8,128)}), f32[5120,128]{1,0:T(8,128)}) %all-gather.12.cloned.1.call-update) | async-done | bytes 2621456 | tf_op jit(solution)/shard_map/all_gather | solution.py:57
  397.1 15.3 %multiply_reduce_fusion.2 = (f32[128]{0:T(128)S(1)}, f32[128]{0:T(128)S(1)}, f32[320,128]{1,0:T(8,128)S(1)}) fusion(f32[320,128]{1,0:T(8,128)} %fusion.16, f32[5120,128]{1,0:T(8,128)} %all-gather.12.cloned.1.call-done, f32[320,5120]{0,1:T(8,128)} %all-gather.8.cloned.1.call-done, s32[320]{0:T(512)S(1)} %iota_add_fusion), kind=kOutput, calls=%fused_computation.32 | convolution fusion | flops 2521661184 | bytes 9505024 | tf_op jit(solution)/shard_map/dot_general | solution.py:55
  412.4 38.2 %all-reduce = (f32[128]{0:T(128)S(1)}, f32[128]{0:T(128)S(1)}) all-reduce(f32[128]{0:T(128)S(1)} %get-tuple-element.6, f32[128]{0:T(128)S(1)} %get-tuple-element.5), channel_id=1, replica_groups=mesh['dp'=16,'mp'=8] {'dp'}, use_global_device_ids=true, to_apply=%region_4.5 | all-reduce | flops 256 | bytes 2048 | tf_op jit(solution)/shard_map/psum | solution.py:62
  450.7 0.0 copy-done
  450.7 0.1 multiply_reduce_fusion.1
  450.7 35.7 %psum.30 = f32[128]{0:T(128)S(1)} all-reduce(f32[128]{0:T(128)S(1)} %multiply_reduce_fusion.1), channel_id=1, replica_groups=mesh['dp'=16,'mp'=8] {'dp'}, use_global_device_ids=true, to_apply=%region_8.9 | all-reduce | flops 128 | bytes 1024 | tf_op jit(solution)/shard_map/psum | solution.py:62
  486.5 0.7 multiply_add_fusion.1
  487.2 0.0 copy-start.1
  487.2 0.0 all-gather.14.cloned.1.call-update
  487.2 44.2 %all-gather.14.cloned.1.call-done = f32[5120,128]{1,0:T(8,128)} async-done(((f32[320,128]{1,0:T(8,128)}), f32[5120,128]{1,0:T(8,128)}) %all-gather.14.cloned.1.call-update) | async-done | bytes 2621456 | tf_op jit(solution)/shard_map/all_gather | solution.py:57
  531.4 15.3 %fusion.18 = f32[128]{0:T(128)S(1)} fusion(f32[320,128]{1,0:T(8,128)} %multiply_add_fusion.1, f32[5120,128]{1,0:T(8,128)} %all-gather.14.cloned.1.call-done, f32[320,5120]{0,1:T(8,128)} %all-gather.8.cloned.1.call-done, s32[320]{0:T(512)S(1)} %iota_add_fusion), kind=kOutput, calls=%fused_computation.26 | convolution fusion | flops 2521579520 | bytes 9340672 | tf_op jit(solution)/shard_map/dot_general | solution.py:55
  546.8 38.2 %psum.31 = f32[128]{0:T(128)S(1)} all-reduce(f32[128]{0:T(128)S(1)} %fusion.18), channel_id=1, replica_groups=mesh['dp'=16,'mp'=8] {'dp'}, use_global_device_ids=true, to_apply=%region_10.11 | all-reduce | flops 128 | bytes 1024 | tf_op jit(solution)/shard_map/psum | solution.py:70
  585.0 0.0 copy-done.1
  585.0 0.7 multiply_add_fusion
  (5 shorter events, 0.1 us)
Async XLA Ops:
  6.5 61.9 %all-gather.6.cloned.1.call-start = ((), (), s32[]{:S(2)}) async-start(), calls=%async_computation.1 | async-start | bytes 5570560 | tf_op jit(solution)/shard_map/all_gather | solution.py:23
  7.3 230.8 %reduce-scatter.4.cloned.1.call-start = ((), (), s32[]{:S(2)}) async-start(), calls=%async_computation.6 | async-start | bytes 16711680 | tf_op jit(solution)/shard_map/reduce_scatter | solution.py:39
  132.5 1.0 copy-start.2
  132.6 153.4 %all-gather.10.cloned.1.call-start = ((), (), s32[]{:S(2)}) async-start(), calls=%async_computation.3 | async-start | bytes 2785280 | tf_op jit(solution)/shard_map/all_gather | solution.py:57
  134.3 200.1 %all-gather.8.cloned.1.call-start = ((), (), s32[]{:S(2)}) async-start(), calls=%async_computation.2 | async-start | bytes 8847360 | tf_op jit(solution)/shard_map/all_gather | solution.py:47
  240.6 156.5 %all-gather.12.cloned.1.call-start = ((), (), s32[]{:S(2)}) async-start(), calls=%async_computation.4 | async-start | bytes 2785280 | tf_op jit(solution)/shard_map/all_gather | solution.py:57
  350.3 100.3 %copy-start = (f32[320,128]{1,0:T(8,128)S(1)}, f32[320,128]{1,0:T(8,128)}, u32[]{:S(2)}) copy-start(f32[320,128]{1,0:T(8,128)} %fusion.16) | copy-start | bytes 491524
  350.3 181.1 %all-gather.14.cloned.1.call-start = ((), (), s32[]{:S(2)}) async-start(), calls=%async_computation.5 | async-start | bytes 2785280 | tf_op jit(solution)/shard_map/all_gather | solution.py:57
  487.2 97.8 %copy-start.1 = (f32[320,128]{1,0:T(8,128)S(1)}, f32[320,128]{1,0:T(8,128)}, u32[]{:S(2)}) copy-start(f32[320,128]{1,0:T(8,128)} %multiply_add_fusion.1) | copy-start | bytes 491524
Sparse Core Ops, SparseCore 0:
  9.5 58.9 all-gather.5
  132.7 105.3 reduce-scatter.3
  240.5 45.4 all-gather.9
  287.6 46.6 all-gather.7
  350.5 46.5 all-gather.11
  487.3 44.0 all-gather.13
where the time goes:
time: 593 us
  waiting for transfers between devices  320 us (54%)
  blocking collectives  112 us (19%)
  matrix products  92.8 us (16%)
  other arithmetic  32.6 us (5%)
  local copies, waits for them, and re-layouts  21.2 us (4%)
  between operations  13.5 us (2%)
    all_gather x3, waiting for transfers between devices, apply(): lax.all_gather(vector, 'dp', axis=0, tiled=True)  136 us
    reduce_scatter x1, waiting for transfers between devices, shards(): lax.psum_scatter(jnp.concatenate([gram_part, (ALPHA * cross + (1.0 - ALPH...  104 us
    psum x2, blocking collectives, norm_of(): return lax.psum(column_sum(residual, residual), 'dp')  73.9 us
    all_gather x1, waiting for transfers between devices, shards(): gram_rows = lax.all_gather(gram_block, 'mp', axis=1, tiled=True)  48.4 us
    dot_general x3, matrix products, apply(): jnp.dot(operator, lax.all_gather(vector, 'dp', axis=0, tiled=True), preci...  46.6 us
    psum x1, blocking collectives, shards(): alpha = norm_now / lax.psum(column_sum(direction, image), 'dp')  38.2 us
    all_gather x1, waiting for transfers between devices, shards(): full_weights = lax.all_gather(task_weights, 'dp', axis=1, tiled=True)  30.8 us
    dot_general x1, matrix products, shards(): jnp.einsum('tnk,tnc->kc', rows_x, outputs, preferred_element_type=jnp.flo...  24.6 us
  transfers between devices with their start and end apart: 6, of which 6 were waited for; matrix products, arithmetic and copies ran while one was open for 6% of the time, Pallas kernels for 0%

commit v1 on v0

v1 whole, which is shorter than its diff:
```python
import functools

import jax
import jax.numpy as jnp
from jax import lax
from jax.experimental import pallas as pl
from jax.experimental.pallas import tpu as pltpu
from jax.sharding import PartitionSpec as P

ALPHA = 0.9
SIDE = 4
CHUNK = 512
F32 = jnp.float32
BF16 = jnp.bfloat16
ALL = ("dp", "mp")


def mat(left, right):
    return lax.dot_general(left, right, (((1,), (0,)), ((), ())), preferred_element_type=F32)


def mat_t(left, right):
    return lax.dot_general(left, right, (((0,), (0,)), ((), ())), preferred_element_type=F32)


def split(value):
    high = value.astype(BF16)
    return high, (value - high.astype(F32)).astype(BF16)


def block(i, size):
    return pl.ds(pl.multiple_of(i * size, size), size)


def load_kernel(x_hbm, x_ref, squares_ref, flat, sem):
    tasks, width = flat.shape
    owners = squares_ref.shape[0]
    local, rows_own = x_ref.shape[0] // tasks, width // owners
    copies = []
    for t in range(tasks):
        copies.append(
            pltpu.make_async_copy(x_hbm.at[t], x_ref.at[pl.ds(t * local, local)], sem.at[t])
        )
        copies[-1].start()
    for t, copy in enumerate(copies):
        copy.wait()

        def body(j, carry, t=t):
            cols = block(j, CHUNK)
            part = x_ref[t * local : (t + 1) * local, cols].astype(F32)
            flat[t : t + 1, cols] = jnp.sum(part * part, axis=0, keepdims=True)
            return carry

        lax.fori_loop(0, width // CHUNK, body, 0)
    squares_ref[...] = jnp.zeros_like(squares_ref)
    lanes = squares_ref.shape[2]
    for j in range(owners):
        for k, at in enumerate(range(0, rows_own, lanes)):
            size = min(lanes, rows_own - at)
            squares_ref[j, k * tasks : (k + 1) * tasks, :size] = flat[
                :, j * rows_own + at : j * rows_own + at + size
            ]


def token_sums(scale, x_ref, z, out_ref):
    owners, _, lanes = out_ref.shape
    rows_own = x_ref.shape[1] // owners
    for j in range(0, owners, 2):
        both = mat_t(x_ref[:, j * rows_own : (j + 2) * rows_own], z[...])
        both = ((both[:, :lanes] + both[:, lanes:]) * scale).astype(BF16)
        out_ref[j, :rows_own] = both[:rows_own]
        out_ref[j + 1, :rows_own] = both[rows_own:]


def fill(w_ref, blocks, sem):
    copies = []
    for i, (piece, across, along) in enumerate(blocks):
        rows_own = piece.shape[1]
        copies.append(
            pltpu.make_async_copy(
                piece, w_ref.at[:, block(owner(across, along), rows_own)], sem.at[i]
            )
        )
        copies[-1].start()
    for copy in copies:
        copy.wait()


def mean_of(tasks, w_ref, rows):
    total = w_ref[0, rows, :].astype(F32)
    for t in range(1, tasks):
        total = total + w_ref[t, rows, :].astype(F32)
    return total / tasks


def products(tasks, x_ref, w_ref, mean, units):
    lanes = w_ref.shape[2]
    size = mean.shape[0] // len(units)
    for i, unit in enumerate(units):
        high, low = split(mean_of(tasks, w_ref, block(unit, size)))
        mean[i * size : (i + 1) * size, :lanes] = high
        mean[i * size : (i + 1) * size, lanes:] = low
    local = x_ref.shape[0] // tasks
    for t in range(tasks):
        rows = slice(t * local, (t + 1) * local)
        both, rest = 0.0, 0.0
        for i, unit in enumerate(units):
            cols, at = block(unit, size), slice(i * size, (i + 1) * size)
            right = jnp.concatenate([w_ref[t, cols, :], mean[at, :lanes]], axis=1)
            both = both + mat(x_ref[rows, cols], right)
            rest = rest + mat(x_ref[rows, cols], mean[at, lanes:])
        yield rows, both[:, :lanes], both[:, lanes:] + rest


def prepare_kernel(tasks, x_ref, *refs):
    *pieces, part_ref, w_ref, mean, sem = refs
    own, line, pairs = pieces[0], pieces[1:SIDE], pieces[SIDE:]
    blocks = [(own, 0, 0)] + [(piece, 0, k + 1) for k, piece in enumerate(line)]
    for i, pair in enumerate(pairs):
        blocks += [(pair.at[k], (1, 3)[i // 2], i % 2 * 2 + k) for k in range(2)]
    fill(w_ref, blocks, sem)
    lanes = w_ref.shape[2]
    for rows, outputs, shift in products(tasks, x_ref, w_ref, mean, units(False)):
        part_ref[rows, :lanes] = outputs
        part_ref[rows, lanes:] = shift


def first_kernel(
    scale, tasks, x_ref, squares_ref, part_ref, w_in, near_ref, wide_ref, out_ref, w_ref, mean, z, sem
):
    del w_in
    blocks = [(piece.at[k], 2, i * 2 + k) for i, piece in enumerate((near_ref, wide_ref)) for k in range(2)]
    fill(w_ref, blocks, sem)
    lanes = out_ref.shape[2]
    for rows, outputs, shift in products(tasks, x_ref, w_ref, mean, units(True)):
        outputs = outputs + part_ref[rows, :lanes]
        shift = shift + part_ref[rows, lanes:]
        high, low = split(outputs.astype(BF16).astype(F32) - shift)
        z[rows, :lanes] = high
        z[rows, lanes:] = low
    token_sums(scale, x_ref, z, out_ref)
    out_ref[:, x_ref.shape[1] // out_ref.shape[0] :] = squares_ref[...].astype(BF16)


def apply_kernel(scale, x_ref, v_ref, out_ref, u_ref, z):
    for i in range(0, x_ref.shape[0], CHUNK):
        rows = slice(i, i + CHUNK)
        u = mat(x_ref[rows, :], v_ref[...])
        u_ref[rows, :] = u
        z[:, rows] = u.T.astype(BF16)
    rows_own = x_ref.shape[1] // out_ref.shape[0]
    for j in range(0, out_ref.shape[0], 2):
        both = mat(z[...], x_ref[:, j * rows_own : (j + 2) * rows_own])
        both = (both * scale).T.astype(BF16)
        out_ref[j] = both[:rows_own]
        out_ref[j + 1] = both[rows_own:]


def sum_parts(parts_ref):
    total = parts_ref[0].astype(F32)
    for j in range(1, parts_ref.shape[0]):
        total = total + parts_ref[j].astype(F32)
    return total


def residual_kernel(total, parts_ref, w_ref, residual_ref, diag_ref, start_ref, out_ref):
    tasks, rows_own, lanes = w_ref.shape
    summed = sum_parts(parts_ref)
    columns = (summed[rows_own:] / total).T
    mean = w_ref[0].astype(F32)
    for t in range(1, tasks):
        mean = mean + w_ref[t].astype(F32)
    mean = mean / tasks
    for k, at in enumerate(range(0, rows_own, lanes)):
        rows = slice(at, min(at + lanes, rows_own))
        size = rows.stop - rows.start
        diag = jnp.zeros((size, lanes), F32)
        own = jnp.zeros((size, lanes), F32)
        for t in range(tasks):
            column = columns[:size, k * tasks + t : k * tasks + t + 1]
            diag = diag + jnp.broadcast_to(column, diag.shape)
            own = own + column * (w_ref[t, rows].astype(F32) - mean[rows])
        residual = summed[rows] + (1.0 - ALPHA) * own
        residual_ref[rows] = residual
        diag_ref[rows] = diag
        for j in range(out_ref.shape[0]):
            out_ref[j, rows] = residual.astype(BF16)
    start_ref[...] = mean


def image_kernel(parts_ref, residual_ref, diag_ref, image_ref, out_ref):
    residual = residual_ref[...]
    lost = residual - residual.astype(BF16).astype(F32)
    image = sum_parts(parts_ref) + diag_ref[...] * ((1.0 - ALPHA) * residual + ALPHA * lost)
    image_ref[...] = image
    for j in range(out_ref.shape[0]):
        out_ref[j] = image.astype(BF16)


def last_kernel(
    scale, x_ref, u_ref, r_ref, q_ref, residual_ref, image_ref, diag_ref, direction_ref, scal_ref, out_ref, v
):
    for i in range(0, x_ref.shape[0], CHUNK):
        v[i : i + CHUNK, :] = mat(x_ref[i : i + CHUNK, :], q_ref[...])
    r = r_ref[...].astype(F32)
    q = q_ref[...].astype(F32)
    norm = jnp.sum(r * r, axis=0, keepdims=True)
    alpha = norm / jnp.sum(r * q, axis=0, keepdims=True)
    r = r_ref[...].astype(F32) - alpha * q_ref[...].astype(F32)
    norm_next = jnp.sum(r * r, axis=0, keepdims=True)
    beta = norm_next / norm
    residual = residual_ref[...]
    direction = residual - alpha * image_ref[...] + beta * residual
    direction_ref[...] = direction
    scal_ref[...] = jnp.zeros_like(scal_ref)
    scal_ref[0:1, :] = alpha
    scal_ref[1:2, :] = norm_next
    shape = scal_ref.shape
    along = (1.0 + beta) * u_ref[...] - alpha * v[...]
    own = jnp.sum((diag_ref[...] * direction * direction).reshape(-1, *shape), axis=0)
    curve = scale * jnp.sum((along * along).reshape(-1, *shape), axis=0) + (1.0 - ALPHA) * own
    for j in range(out_ref.shape[0]):
        out_ref[j] = curve


def merge_kernel(parts_ref, scal_ref, start_ref, residual_ref, direction_ref, out_ref):
    curve = jnp.sum(sum_parts(parts_ref), axis=0, keepdims=True)
    out_ref[...] = (
        start_ref[...]
        + scal_ref[0:1, :] * residual_ref[...]
        + scal_ref[1:2, :] / curve * direction_ref[...]
    )


def call(kernel, name, scratch, out_shape, *args, place=pltpu.VMEM, n_vmem=1, aliases=None):
    vmem = pl.BlockSpec(memory_space=pltpu.VMEM)
    return pl.pallas_call(
        kernel,
        name=name,
        in_specs=[vmem] * n_vmem + [pl.BlockSpec(memory_space=place)] * (len(args) - n_vmem),
        out_specs=jax.tree.map(lambda _: vmem, out_shape),
        out_shape=out_shape,
        scratch_shapes=scratch,
        input_output_aliases=aliases or {},
        compiler_params=pltpu.CompilerParams(vmem_limit_bytes=10 << 20),
    )(*args)


def place():
    dp, odd = lax.axis_index("dp"), lax.axis_index("mp") % 2
    y, z = dp // SIDE, dp % SIDE
    return odd, jnp.where(odd == 0, y, z), jnp.where(odd == 0, z, y)


def owner(across, along):
    odd, at_across, at_along = place()
    a = (at_across - across + SIDE) % SIDE
    b = (at_along - along + SIDE) % SIDE
    return jnp.where(odd == 0, a * SIDE + b, b * SIDE + a)


def units(late):
    odd, across, _ = place()
    far = (across + 2) % SIDE
    even_units = []
    for base in (across, far) if late else ((across + 1) % SIDE, (across + 3) % SIDE):
        even_units += [2 * base, 2 * base + 1]
    pair = far // 2 if late else 1 - far // 2
    return [jnp.where(odd == 0, even_units[i], 2 * i + pair) for i in range(SIDE)]


def send(value, n_cols, across, along):
    pairs = []
    for dp in range(SIDE * SIDE):
        for mp in range(n_cols):
            step_y, step_z = (across, along) if mp % 2 == 0 else (along, across)
            y, z = (dp // SIDE + step_y) % SIDE, (dp % SIDE + step_z) % SIDE
            pairs.append((dp * n_cols + mp, (y * SIDE + z) * n_cols + mp))
    return lax.ppermute(value, ALL, pairs)


def shards(activations, task_weights):
    tasks, local, width = activations.shape
    lanes = task_weights.shape[2]
    n_rows, n_cols = lax.axis_size("dp"), lax.axis_size("mp")
    rows_own = width // n_rows
    tokens = tasks * local
    total = tokens * n_rows

    def exchange(value):
        return lax.all_to_all(value, "dp", 0, 0, tiled=False)

    scale = ALPHA / total
    unit = pltpu.VMEM((width // 2, 2 * lanes), BF16)
    halves = pltpu.VMEM((tokens, 2 * lanes), BF16)
    rows = jax.ShapeDtypeStruct((rows_own, lanes), F32)
    copies = jax.ShapeDtypeStruct((n_rows, rows_own, lanes), BF16)
    small = jax.ShapeDtypeStruct((8, lanes), F32)
    extra = 2 * 8
    line = [send(task_weights, n_cols, 0, k) for k in range(1, SIDE)]
    vmem = pl.BlockSpec(memory_space=pltpu.VMEM)
    x, squares = pl.pallas_call(
        load_kernel,
        name="load",
        in_specs=[pl.BlockSpec(memory_space=pltpu.HBM)],
        out_specs=(vmem, vmem),
        out_shape=(
            pltpu.VMEM((tokens, width), BF16),
            jax.ShapeDtypeStruct((n_rows, extra, lanes), F32),
        ),
        scratch_shapes=[pltpu.VMEM((tasks, width), F32), pltpu.SemaphoreType.DMA((tasks,))],
        compiler_params=pltpu.CompilerParams(vmem_limit_bytes=4 << 20),
    )(pltpu.with_memory_space_constraint(activations, pltpu.HBM))
    *line, squares = lax.optimization_barrier((*line, squares))
    near, wide = jnp.stack([task_weights, line[0]]), jnp.stack(line[1:])
    left_near = send(near, n_cols, 1, 0)
    right_wide = send(wide, n_cols, 3, 0)
    left_wide = send(wide, n_cols, 1, 0)
    right_near = send(near, n_cols, 3, 0)
    far_near = send(left_near, n_cols, 1, 0)
    far_wide = send(right_wide, n_cols, 3, 0)
    part, w = call(
        functools.partial(prepare_kernel, tasks),
        "prepare",
        [unit, pltpu.SemaphoreType.DMA((n_rows - SIDE,))],
        (
            jax.ShapeDtypeStruct((tokens, 2 * lanes), F32),
            jax.ShapeDtypeStruct((tasks, width, lanes), BF16),
        ),
        x,
        task_weights,
        *line,
        left_near,
        left_wide,
        right_near,
        right_wide,
        place=pl.ANY,
    )
    part, _ = call(
        functools.partial(first_kernel, scale, tasks),
        "first",
        [unit, halves, pltpu.SemaphoreType.DMA((SIDE,))],
        (
            jax.ShapeDtypeStruct((n_rows, rows_own + extra, lanes), BF16),
            jax.ShapeDtypeStruct((tasks, width, lanes), BF16),
        ),
        x,
        squares,
        part,
        w,
        far_near,
        far_wide,
        place=pl.ANY,
        n_vmem=4,
        aliases={3: 1},
    )
    residual, diag, start, sent = call(
        functools.partial(residual_kernel, total),
        "residual",
        [],
        (rows, rows, rows, copies),
        exchange(part),
        task_weights,
    )
    r_full = exchange(sent).reshape(width, lanes)
    part, u = call(
        functools.partial(apply_kernel, scale),
        "apply",
        [pltpu.VMEM((lanes, tokens), BF16)],
        (copies, jax.ShapeDtypeStruct((tokens, lanes), F32)),
        x,
        r_full,
    )
    image, sent = call(image_kernel, "image", [], (rows, copies), exchange(part), residual, diag)
    q_full = exchange(sent).reshape(width, lanes)
    direction, scal, curve = call(
        functools.partial(last_kernel, scale),
        "last",
        [pltpu.VMEM((tokens, lanes), F32)],
        (rows, small, jax.ShapeDtypeStruct((n_rows, 8, lanes), F32)),
        x,
        u,
        r_full,
        q_full,
        residual,
        image,
        diag,
    )
    return call(
        merge_kernel, "merge", [], rows, exchange(curve), scal, start, residual, direction
    )


def solution(mesh):
    return jax.shard_map(
        shards,
        mesh=mesh,
        in_specs=(P(None, "dp", None), P(None, "dp", "mp")),
        out_specs=P("dp", "mp"),
        check_vma=False,
    )
```

time: 593 us -> 162 us (0.27)
  waiting for transfers between devices: 320 us -> 13.7 us
  matrix products: 92.8 us -> 0 us
  Pallas kernels: 0 us -> 43.9 us
  other arithmetic: 32.6 us -> 0.12 us
  blocking collectives: 112 us -> 89.6 us
  local copies, waits for them, and re-layouts: 21.2 us -> 0.01 us
  between operations: 13.5 us -> 0.09 us
  starting transfers between devices: 0.61 us -> 14 us
    all_gather x5 -> x0, waiting for transfers between devices: 215 us -> none  [the longest x3 136 us: apply(): lax.all_gather(vector, 'dp', axis=0, tiled=True)]
    psum x3 -> x0, blocking collectives: 112 us -> none  [the longest x2 73.9 us: norm_of(): return lax.psum(column_sum(residual, residual), 'dp')]
    reduce_scatter x1 -> x0, waiting for transfers between devices: 104 us -> none  [shards(): lax.psum_scatter(jnp.concatenate([gram_part, (ALPHA * cross + (1.0 - ALPH...]
    dot_general x5 -> x0, matrix products: 92.8 us -> none  [the longest x3 46.6 us: apply(): jnp.dot(operator, lax.all_gather(vector, 'dp', axis=0, tiled=True), preci...]
    all_to_all x0 -> x5, blocking collectives: none -> 89.6 us  [exchange(): return lax.all_to_all(value, 'dp', 0, 0, tiled=False)]
    pallas_call x0 -> x8, Pallas kernels: none -> 43.9 us  [the longest x7 36.3 us: call(): pl.pallas_call(kernel, name=name, in_specs=[vmem] * n_vmem + [pl.BlockSpe...]
    unnamed x8 -> x2, local copies, waits for them, and re-layouts: 17.9 us -> 0.01 us
    ppermute x0 -> x9, starting transfers between devices: none -> 14 us  [send(): return lax.ppermute(value, ALL, pairs)]
  transfers between devices with their start and end apart: 6 -> 9, of which waited for: 6 -> 4; matrix products, arithmetic and copies ran while one was open for 6% -> 0% of each run, Pallas kernels for 0% -> 9%
where the time goes in v1:
time: 162 us
  blocking collectives  89.6 us (55%)
  Pallas kernels  43.9 us (27%)
  starting transfers between devices  14 us (9%)
  waiting for transfers between devices  13.7 us (8%)
    all_to_all x5, blocking collectives, exchange(): return lax.all_to_all(value, 'dp', 0, 0, tiled=False)  89.6 us
    pallas_call x7, Pallas kernels, call(): pl.pallas_call(kernel, name=name, in_specs=[vmem] * n_vmem + [pl.BlockSpe...  36.3 us
    ppermute x9, starting transfers between devices, send(): return lax.ppermute(value, ALL, pairs)  14 us
    ppermute x9, waiting for transfers between devices, send(): return lax.ppermute(value, ALL, pairs)  13.7 us
    pallas_call x1, Pallas kernels, shards(): pl.pallas_call(load_kernel, name='load', in_specs=[pl.BlockSpec(memory_sp...  7.68 us
  transfers between devices with their start and end apart: 9, of which 4 were waited for; matrix products, arithmetic and copies ran while one was open for 0% of the time, Pallas kernels for 9%

profile of v1, /device:TPU:0, one launch (start us, length us, event | category | flops | bytes accessed | tf_op | source)
XLA Modules:
  0.0 161.5 jit_solution(4529697723540826206)
XLA Ops:
  0.0 0.0 copy-start
  0.0 4.1 %collective-permute-start.2 = (bf16[4,320,128]{2,1,0:T(8,128)(2,1)}, bf16[4,320,128]{2,1,0:T(8,128)(2,1)S(1)}, u32[]{:S(2)}, u32[]{:S(2)}) collective-permute-start(bf16[4,320,128]{2,1,0:T(8,128)(2,1)} %w_ref.1), channel_id=1, source_target_pairs={{0,24},{1,97},{2,26},{3,99},{4,28},{5,101},{6,30},{7,103},{8,0},{9... | collective-permute-start | bytes 983048 | tf_op jit(solution)/shard_map/ppermute | solution.py:279
  4.1 0.0 collective-permute-start.1
  4.1 1.3 collective-permute-start
  5.4 7.7 %load.1 = (bf16[2048,5120]{1,0:T(8,128)(2,1)S(1)}, f32[16,16,128]{2,1,0:T(8,128)S(1)}) custom-call(bf16[4,512,5120]{2,1,0:T(8,128)(2,1)} %x_hbm.1), custom_call_target="tpu_custom_call" | custom-call | tf_op jit(solution)/shard_map/load/pallas_call | solution.py:302
  13.1 0.0 collective-permute-done.2.refs_3_
  13.1 0.0 collective-permute-done.1.refs_2_
  13.1 3.0 %collective-permute-done.refs_1_ = bf16[4,320,128]{2,1,0:T(8,128)(2,1)S(1)} collective-permute-done((bf16[4,320,128]{2,1,0:T(8,128)(2,1)}, bf16[4,320,128]{2,1,0:T(8,128)(2,1)S(1)}, u32[]{:S(2)}, u32[]{:S(2)}) %collective-permute-start) | collective-permute-done | bytes 327712 | tf_op jit(solution)/shard_map/ppermute | solution.py:279
  16.1 0.0 copy-done
  16.1 0.1 pad_maximum_fusion
  16.2 1.6 %collective-permute-start.3 = (bf16[2,4,320,128]{3,2,1,0:T(8,128)(2,1)S(1)}, bf16[2,4,320,128]{3,2,1,0:T(8,128)(2,1)S(1)}, u32[]{:S(2)}, u32[]{:S(2)}) collective-permute-start(bf16[2,4,320,128]{3,2,1,0:T(8,128)(2,1)S(1)} %pad_maximum_fusion), channel_id=1, source_target_pairs={{0,32},{1,9},{2,34},{3,11},{4,36},{5,13},{6,38},{7,15},{8,40},{9,1... | collective-permute-start | bytes 1966088 | tf_op jit(solution)/shard_map/ppermute | solution.py:279
  17.8 0.1 pad_maximum_fusion.1
  17.9 1.7 %collective-permute-start.6 = (bf16[2,4,320,128]{3,2,1,0:T(8,128)(2,1)S(1)}, bf16[2,4,320,128]{3,2,1,0:T(8,128)(2,1)S(1)}, u32[]{:S(2)}, u32[]{:S(2)}) collective-permute-start(bf16[2,4,320,128]{3,2,1,0:T(8,128)(2,1)S(1)} %pad_maximum_fusion.1), channel_id=1, source_target_pairs={{0,96},{1,25},{2,98},{3,27},{4,100},{5,29},{6,102},{7,31},{8,104},... | collective-permute-start | bytes 1966088 | tf_op jit(solution)/shard_map/ppermute | solution.py:279
  19.6 1.8 %collective-permute-start.5 = (bf16[2,4,320,128]{3,2,1,0:T(8,128)(2,1)S(1)}, bf16[2,4,320,128]{3,2,1,0:T(8,128)(2,1)S(1)}, u32[]{:S(2)}, u32[]{:S(2)}) collective-permute-start(bf16[2,4,320,128]{3,2,1,0:T(8,128)(2,1)S(1)} %pad_maximum_fusion), channel_id=1, source_target_pairs={{0,96},{1,25},{2,98},{3,27},{4,100},{5,29},{6,102},{7,31},{8,104},... | collective-permute-start | bytes 1966088 | tf_op jit(solution)/shard_map/ppermute | solution.py:279
  21.4 0.2 collective-permute-start.4
  21.7 6.4 %collective-permute-done.3.refs_4_ = bf16[2,4,320,128]{3,2,1,0:T(8,128)(2,1)S(1)} collective-permute-done((bf16[2,4,320,128]{3,2,1,0:T(8,128)(2,1)S(1)}, bf16[2,4,320,128]{3,2,1,0:T(8,128)(2,1)S(1)}, u32[]{:S(2)}, u32[]{:S(2)}) %collective-permute-start.3) | collective-permute-done | bytes 655392 | tf_op jit(solution)/shard_map/ppermute | solution.py:279
  28.1 0.4 collective-permute-start.7
  28.4 0.1 collective-permute-done.6.refs_7_
  28.6 2.9 %collective-permute-start.8 = (bf16[2,4,320,128]{3,2,1,0:T(8,128)(2,1)S(1)}, bf16[2,4,320,128]{3,2,1,0:T(8,128)(2,1)S(1)}, u32[]{:S(2)}, u32[]{:S(2)}) collective-permute-start(bf16[2,4,320,128]{3,2,1,0:T(8,128)(2,1)S(1)} %collective-permute-done.6.refs_7_), channel_id=1, source_target_pairs={{0,96},{1,25},{2,98},{3,27},{4,100},{5,29},{6,102},{7,31},{8,104},... | collective-permute-start | bytes 1966088 | tf_op jit(solution)/shard_map/ppermute | solution.py:279
  31.4 4.2 %collective-permute-done.5.refs_6_ = bf16[2,4,320,128]{3,2,1,0:T(8,128)(2,1)S(1)} collective-permute-done((bf16[2,4,320,128]{3,2,1,0:T(8,128)(2,1)S(1)}, bf16[2,4,320,128]{3,2,1,0:T(8,128)(2,1)S(1)}, u32[]{:S(2)}, u32[]{:S(2)}) %collective-permute-start.5) | collective-permute-done | bytes 655392 | tf_op jit(solution)/shard_map/ppermute | solution.py:279
  35.6 0.0 collective-permute-done.4.refs_5_
  35.6 7.2 %prepare.1 = (f32[2048,256]{1,0:T(8,128)S(1)}, bf16[4,5120,128]{2,1,0:T(8,128)(2,1)S(1)}) custom-call(bf16[2048,5120]{1,0:T(8,128)(2,1)S(1)} %get-tuple-element.25.x_ref, bf16[4,320,128]{2,1,0:T(8,128)(2,1)S(1)} %copy-done, bf16[4,320,128]{2,1,0:T(8,128)(2,1)S(1)} %collective-permute-done.refs_1_, bf16[4,320,128]{2,1,0:T(8,128)(2,1)S(1)} %collective-permute-done.1.refs_2_, ...), custom_call_target="tpu_custom_call" | custom-call | tf_op jit(solution)/shard_map/prepare/pallas_call | solution.py:237
  42.8 0.0 collective-permute-done.7.near_ref
  42.8 0.0 collective-permute-done.8.wide_ref
  42.8 12.5 %first.1 = (bf16[16,336,128]{2,1,0:T(8,128)(2,1)S(1)}, bf16[4,5120,128]{2,1,0:T(8,128)(2,1)S(1)}) custom-call(bf16[2048,5120]{1,0:T(8,128)(2,1)S(1)} %get-tuple-element.25.x_ref, f32[16,16,128]{2,1,0:T(8,128)S(1)} %get-tuple-element.27.squares_ref, f32[2048,256]{1,0:T(8,128)S(1)} %get-tuple-element.31.part_ref, ...), custom_call_target="tpu_custom_call", output_to_operand_aliasing={{1}: (3, {})} | custom-call | tf_op jit(solution)/shard_map/first/pallas_call | solution.py:237
  55.3 22.6 %all_to_all.25.parts_ref = bf16[16,336,128]{2,1,0:T(8,128)(2,1)S(1)} all-to-all(bf16[16,336,128]{2,1,0:T(8,128)(2,1)S(1)} %get-tuple-element.33), channel_id=1, replica_groups=mesh['dp'=16,'mp'=8] {'dp'}, dimensions={0} | all-to-all | bytes 2752512 | tf_op jit(solution)/shard_map/all_to_all | solution.py:291
  77.9 0.5 residual.1
  78.4 19.8 %all_to_all.26 = bf16[16,320,128]{2,1,0:T(8,128)(2,1)S(1)} all-to-all(bf16[16,320,128]{2,1,0:T(8,128)(2,1)S(1)} %get-tuple-element.34), channel_id=1, replica_groups=mesh['dp'=16,'mp'=8] {'dp'}, dimensions={0} | all-to-all | bytes 2621440 | tf_op jit(solution)/shard_map/all_to_all | solution.py:291
  98.2 9.2 %apply.1 = (bf16[16,320,128]{2,1,0:T(8,128)(2,1)S(1)}, f32[2048,128]{1,0:T(8,128)S(1)}) custom-call(bf16[2048,5120]{1,0:T(8,128)(2,1)S(1)} %get-tuple-element.25.x_ref, bf16[5120,128]{1,0:T(8,128)(2,1)S(1)} %bitcast.6), custom_call_target="tpu_custom_call" | custom-call | tf_op jit(solution)/shard_map/apply/pallas_call | solution.py:237
  107.4 18.6 %all_to_all.27.parts_ref = bf16[16,320,128]{2,1,0:T(8,128)(2,1)S(1)} all-to-all(bf16[16,320,128]{2,1,0:T(8,128)(2,1)S(1)} %get-tuple-element.36), channel_id=1, replica_groups=mesh['dp'=16,'mp'=8] {'dp'}, dimensions={0} | all-to-all | bytes 2621440 | tf_op jit(solution)/shard_map/all_to_all | solution.py:291
  126.0 0.3 image.1
  126.3 17.6 %all_to_all.28 = bf16[16,320,128]{2,1,0:T(8,128)(2,1)S(1)} all-to-all(bf16[16,320,128]{2,1,0:T(8,128)(2,1)S(1)} %get-tuple-element.39), channel_id=1, replica_groups=mesh['dp'=16,'mp'=8] {'dp'}, dimensions={0} | all-to-all | bytes 2621440 | tf_op jit(solution)/shard_map/all_to_all | solution.py:291
  143.8 5.9 %last.1 = (f32[320,128]{1,0:T(8,128)S(1)}, f32[8,128]{1,0:T(8,128)S(1)}, f32[16,8,128]{2,1,0:T(8,128)S(1)}) custom-call(bf16[2048,5120]{1,0:T(8,128)(2,1)S(1)} %get-tuple-element.25.x_ref, f32[2048,128]{1,0:T(8,128)S(1)} %get-tuple-element.35.u_ref, bf16[5120,128]{1,0:T(8,128)(2,1)S(1)} %bitcast.7, bf16[5120,128]{1,0:T(8,128)(2,1)S(1)} %bitcast.8, ...), custom_call_target="tpu_custom_call" | custom-call | tf_op jit(solution)/shard_map/last/pallas_call | solution.py:237
  149.7 11.1 %all_to_all.29.parts_ref = f32[16,8,128]{2,1,0:T(8,128)S(1)} all-to-all(f32[16,8,128]{2,1,0:T(8,128)S(1)} %get-tuple-element.41), channel_id=1, replica_groups=mesh['dp'=16,'mp'=8] {'dp'}, dimensions={0} | all-to-all | bytes 131072 | tf_op jit(solution)/shard_map/all_to_all | solution.py:291
  160.8 0.7 merge.1
Async XLA Ops:
  0.0 16.1 %copy-start = (bf16[4,320,128]{2,1,0:T(8,128)(2,1)S(1)}, bf16[4,320,128]{2,1,0:T(8,128)(2,1)}, u32[]{:S(2)}) copy-start(bf16[4,320,128]{2,1,0:T(8,128)(2,1)} %w_ref.1) | copy-start | bytes 983044
  0.0 13.1 %collective-permute-start.2 = (bf16[4,320,128]{2,1,0:T(8,128)(2,1)}, bf16[4,320,128]{2,1,0:T(8,128)(2,1)S(1)}, u32[]{:S(2)}, u32[]{:S(2)}) collective-permute-start(bf16[4,320,128]{2,1,0:T(8,128)(2,1)} %w_ref.1), channel_id=1, source_target_pairs={{0,24},{1,97},{2,26},{3,99},{4,28},{5,101},{6,30},{7,103},{8,0},{9... | collective-permute-start | bytes 983048 | tf_op jit(solution)/shard_map/ppermute | solution.py:279
  4.1 9.0 %collective-permute-start.1 = (bf16[4,320,128]{2,1,0:T(8,128)(2,1)}, bf16[4,320,128]{2,1,0:T(8,128)(2,1)S(1)}, u32[]{:S(2)}, u32[]{:S(2)}) collective-permute-start(bf16[4,320,128]{2,1,0:T(8,128)(2,1)} %w_ref.1), channel_id=1, source_target_pairs={{0,16},{1,65},{2,18},{3,67},{4,20},{5,69},{6,22},{7,71},{8,24},{9,... | collective-permute-start | bytes 983048 | tf_op jit(solution)/shard_map/ppermute | solution.py:279
  4.1 12.0 %collective-permute-start = (bf16[4,320,128]{2,1,0:T(8,128)(2,1)}, bf16[4,320,128]{2,1,0:T(8,128)(2,1)S(1)}, u32[]{:S(2)}, u32[]{:S(2)}) collective-permute-start(bf16[4,320,128]{2,1,0:T(8,128)(2,1)} %w_ref.1), channel_id=1, source_target_pairs={{0,8},{1,33},{2,10},{3,35},{4,12},{5,37},{6,14},{7,39},{8,16},{9,4... | collective-permute-start | bytes 983048 | tf_op jit(solution)/shard_map/ppermute | solution.py:279
  16.2 11.9 %collective-permute-start.3 = (bf16[2,4,320,128]{3,2,1,0:T(8,128)(2,1)S(1)}, bf16[2,4,320,128]{3,2,1,0:T(8,128)(2,1)S(1)}, u32[]{:S(2)}, u32[]{:S(2)}) collective-permute-start(bf16[2,4,320,128]{3,2,1,0:T(8,128)(2,1)S(1)} %pad_maximum_fusion), channel_id=1, source_target_pairs={{0,32},{1,9},{2,34},{3,11},{4,36},{5,13},{6,38},{7,15},{8,40},{9,1... | collective-permute-start | bytes 1966088 | tf_op jit(solution)/shard_map/ppermute | solution.py:279
  17.9 10.7 %collective-permute-start.6 = (bf16[2,4,320,128]{3,2,1,0:T(8,128)(2,1)S(1)}, bf16[2,4,320,128]{3,2,1,0:T(8,128)(2,1)S(1)}, u32[]{:S(2)}, u32[]{:S(2)}) collective-permute-start(bf16[2,4,320,128]{3,2,1,0:T(8,128)(2,1)S(1)} %pad_maximum_fusion.1), channel_id=1, source_target_pairs={{0,96},{1,25},{2,98},{3,27},{4,100},{5,29},{6,102},{7,31},{8,104},... | collective-permute-start | bytes 1966088 | tf_op jit(solution)/shard_map/ppermute | solution.py:279
  19.6 15.9 %collective-permute-start.5 = (bf16[2,4,320,128]{3,2,1,0:T(8,128)(2,1)S(1)}, bf16[2,4,320,128]{3,2,1,0:T(8,128)(2,1)S(1)}, u32[]{:S(2)}, u32[]{:S(2)}) collective-permute-start(bf16[2,4,320,128]{3,2,1,0:T(8,128)(2,1)S(1)} %pad_maximum_fusion), channel_id=1, source_target_pairs={{0,96},{1,25},{2,98},{3,27},{4,100},{5,29},{6,102},{7,31},{8,104},... | collective-permute-start | bytes 1966088 | tf_op jit(solution)/shard_map/ppermute | solution.py:279
  21.4 14.1 %collective-permute-start.4 = (bf16[2,4,320,128]{3,2,1,0:T(8,128)(2,1)S(1)}, bf16[2,4,320,128]{3,2,1,0:T(8,128)(2,1)S(1)}, u32[]{:S(2)}, u32[]{:S(2)}) collective-permute-start(bf16[2,4,320,128]{3,2,1,0:T(8,128)(2,1)S(1)} %pad_maximum_fusion.1), channel_id=1, source_target_pairs={{0,32},{1,9},{2,34},{3,11},{4,36},{5,13},{6,38},{7,15},{8,40},{9,1... | collective-permute-start | bytes 1966088 | tf_op jit(solution)/shard_map/ppermute | solution.py:279
  28.1 14.7 %collective-permute-start.7 = (bf16[2,4,320,128]{3,2,1,0:T(8,128)(2,1)S(1)}, bf16[2,4,320,128]{3,2,1,0:T(8,128)(2,1)S(1)}, u32[]{:S(2)}, u32[]{:S(2)}) collective-permute-start(bf16[2,4,320,128]{3,2,1,0:T(8,128)(2,1)S(1)} %collective-permute-done.3.refs_4_), channel_id=1, source_target_pairs={{0,32},{1,9},{2,34},{3,11},{4,36},{5,13},{6,38},{7,15},{8,40},{9,1... | collective-permute-start | bytes 1966088 | tf_op jit(solution)/shard_map/ppermute | solution.py:279
  28.6 14.2 %collective-permute-start.8 = (bf16[2,4,320,128]{3,2,1,0:T(8,128)(2,1)S(1)}, bf16[2,4,320,128]{3,2,1,0:T(8,128)(2,1)S(1)}, u32[]{:S(2)}, u32[]{:S(2)}) collective-permute-start(bf16[2,4,320,128]{3,2,1,0:T(8,128)(2,1)S(1)} %collective-permute-done.6.refs_7_), channel_id=1, source_target_pairs={{0,96},{1,25},{2,98},{3,27},{4,100},{5,29},{6,102},{7,31},{8,104},... | collective-permute-start | bytes 1966088 | tf_op jit(solution)/shard_map/ppermute | solution.py:279

commit v2 on v1

--- a/solution.py
+++ b/solution.py
@@ -103,13 +103,12 @@
     local = x_ref.shape[0] // tasks
     for t in range(tasks):
         rows = slice(t * local, (t + 1) * local)
-        both, rest = 0.0, 0.0
+        both = 0.0
         for i, unit in enumerate(units):
             cols, at = block(unit, size), slice(i * size, (i + 1) * size)
-            right = jnp.concatenate([w_ref[t, cols, :], mean[at, :lanes]], axis=1)
+            right = jnp.concatenate([w_ref[t, cols, :], mean[at, :]], axis=1)
             both = both + mat(x_ref[rows, cols], right)
-            rest = rest + mat(x_ref[rows, cols], mean[at, lanes:])
-        yield rows, both[:, :lanes], both[:, lanes:] + rest
+        yield rows, both[:, :lanes], both[:, lanes : 2 * lanes] + both[:, 2 * lanes :]
 
 
 def prepare_kernel(tasks, x_ref, *refs):

time: 162 us -> 162 us (level)
  no operation moved by 1% of the time
where the time goes in v2:
time: 162 us; the launch traced here: 161 us
  blocking collectives  89.5 us (55%)
  Pallas kernels  43.8 us (27%)
  starting transfers between devices  14 us (9%)
  waiting for transfers between devices  13.7 us (8%)
    all_to_all x5, blocking collectives, exchange(): return lax.all_to_all(value, 'dp', 0, 0, tiled=False)  89.5 us
    pallas_call x7, Pallas kernels, call(): pl.pallas_call(kernel, name=name, in_specs=[vmem] * n_vmem + [pl.BlockSpe...  36.1 us
    ppermute x9, starting transfers between devices, send(): return lax.ppermute(value, ALL, pairs)  14 us
    ppermute x9, waiting for transfers between devices, send(): return lax.ppermute(value, ALL, pairs)  13.7 us
    pallas_call x1, Pallas kernels, shards(): pl.pallas_call(load_kernel, name='load', in_specs=[pl.BlockSpec(memory_sp...  7.68 us
  transfers between devices with their start and end apart: 9, of which 4 were waited for; matrix products, arithmetic and copies ran while one was open for 0% of the time, Pallas kernels for 9%

profile of v2, /device:TPU:0, one launch (start us, length us, event | category | flops | bytes accessed | tf_op | source)
XLA Modules:
  0.0 161.3 jit_solution(9277819772498559093)
XLA Ops:
  0.0 0.0 copy-start
  0.0 4.1 %collective-permute-start.2 = (bf16[4,320,128]{2,1,0:T(8,128)(2,1)}, bf16[4,320,128]{2,1,0:T(8,128)(2,1)S(1)}, u32[]{:S(2)}, u32[]{:S(2)}) collective-permute-start(bf16[4,320,128]{2,1,0:T(8,128)(2,1)} %w_ref.1), channel_id=1, source_target_pairs={{0,24},{1,97},{2,26},{3,99},{4,28},{5,101},{6,30},{7,103},{8,0},{9... | collective-permute-start | bytes 983048 | tf_op jit(solution)/shard_map/ppermute | solution.py:278
  4.1 0.0 collective-permute-start.1
  4.1 1.3 collective-permute-start
  5.4 7.7 %load.1 = (bf16[2048,5120]{1,0:T(8,128)(2,1)S(1)}, f32[16,16,128]{2,1,0:T(8,128)S(1)}) custom-call(bf16[4,512,5120]{2,1,0:T(8,128)(2,1)} %x_hbm.1), custom_call_target="tpu_custom_call" | custom-call | tf_op jit(solution)/shard_map/load/pallas_call | solution.py:301
  13.1 0.0 collective-permute-done.2.refs_3_
  13.1 0.0 collective-permute-done.1.refs_2_
  13.1 3.0 %collective-permute-done.refs_1_ = bf16[4,320,128]{2,1,0:T(8,128)(2,1)S(1)} collective-permute-done((bf16[4,320,128]{2,1,0:T(8,128)(2,1)}, bf16[4,320,128]{2,1,0:T(8,128)(2,1)S(1)}, u32[]{:S(2)}, u32[]{:S(2)}) %collective-permute-start) | collective-permute-done | bytes 327712 | tf_op jit(solution)/shard_map/ppermute | solution.py:278
  16.1 0.0 copy-done
  16.1 0.1 pad_maximum_fusion
  16.2 1.6 %collective-permute-start.3 = (bf16[2,4,320,128]{3,2,1,0:T(8,128)(2,1)S(1)}, bf16[2,4,320,128]{3,2,1,0:T(8,128)(2,1)S(1)}, u32[]{:S(2)}, u32[]{:S(2)}) collective-permute-start(bf16[2,4,320,128]{3,2,1,0:T(8,128)(2,1)S(1)} %pad_maximum_fusion), channel_id=1, source_target_pairs={{0,32},{1,9},{2,34},{3,11},{4,36},{5,13},{6,38},{7,15},{8,40},{9,1... | collective-permute-start | bytes 1966088 | tf_op jit(solution)/shard_map/ppermute | solution.py:278
  17.8 0.1 pad_maximum_fusion.1
  17.9 1.7 %collective-permute-start.6 = (bf16[2,4,320,128]{3,2,1,0:T(8,128)(2,1)S(1)}, bf16[2,4,320,128]{3,2,1,0:T(8,128)(2,1)S(1)}, u32[]{:S(2)}, u32[]{:S(2)}) collective-permute-start(bf16[2,4,320,128]{3,2,1,0:T(8,128)(2,1)S(1)} %pad_maximum_fusion.1), channel_id=1, source_target_pairs={{0,96},{1,25},{2,98},{3,27},{4,100},{5,29},{6,102},{7,31},{8,104},... | collective-permute-start | bytes 1966088 | tf_op jit(solution)/shard_map/ppermute | solution.py:278
  19.6 1.8 %collective-permute-start.5 = (bf16[2,4,320,128]{3,2,1,0:T(8,128)(2,1)S(1)}, bf16[2,4,320,128]{3,2,1,0:T(8,128)(2,1)S(1)}, u32[]{:S(2)}, u32[]{:S(2)}) collective-permute-start(bf16[2,4,320,128]{3,2,1,0:T(8,128)(2,1)S(1)} %pad_maximum_fusion), channel_id=1, source_target_pairs={{0,96},{1,25},{2,98},{3,27},{4,100},{5,29},{6,102},{7,31},{8,104},... | collective-permute-start | bytes 1966088 | tf_op jit(solution)/shard_map/ppermute | solution.py:278
  21.4 0.2 collective-permute-start.4
  21.7 6.4 %collective-permute-done.3.refs_4_ = bf16[2,4,320,128]{3,2,1,0:T(8,128)(2,1)S(1)} collective-permute-done((bf16[2,4,320,128]{3,2,1,0:T(8,128)(2,1)S(1)}, bf16[2,4,320,128]{3,2,1,0:T(8,128)(2,1)S(1)}, u32[]{:S(2)}, u32[]{:S(2)}) %collective-permute-start.3) | collective-permute-done | bytes 655392 | tf_op jit(solution)/shard_map/ppermute | solution.py:278
  28.1 0.4 collective-permute-start.7
  28.4 0.1 collective-permute-done.6.refs_7_
  28.6 2.9 %collective-permute-start.8 = (bf16[2,4,320,128]{3,2,1,0:T(8,128)(2,1)S(1)}, bf16[2,4,320,128]{3,2,1,0:T(8,128)(2,1)S(1)}, u32[]{:S(2)}, u32[]{:S(2)}) collective-permute-start(bf16[2,4,320,128]{3,2,1,0:T(8,128)(2,1)S(1)} %collective-permute-done.6.refs_7_), channel_id=1, source_target_pairs={{0,96},{1,25},{2,98},{3,27},{4,100},{5,29},{6,102},{7,31},{8,104},... | collective-permute-start | bytes 1966088 | tf_op jit(solution)/shard_map/ppermute | solution.py:278
  31.4 4.2 %collective-permute-done.5.refs_6_ = bf16[2,4,320,128]{3,2,1,0:T(8,128)(2,1)S(1)} collective-permute-done((bf16[2,4,320,128]{3,2,1,0:T(8,128)(2,1)S(1)}, bf16[2,4,320,128]{3,2,1,0:T(8,128)(2,1)S(1)}, u32[]{:S(2)}, u32[]{:S(2)}) %collective-permute-start.5) | collective-permute-done | bytes 655392 | tf_op jit(solution)/shard_map/ppermute | solution.py:278
  35.6 0.0 collective-permute-done.4.refs_5_
  35.6 7.1 %prepare.1 = (f32[2048,256]{1,0:T(8,128)S(1)}, bf16[4,5120,128]{2,1,0:T(8,128)(2,1)S(1)}) custom-call(bf16[2048,5120]{1,0:T(8,128)(2,1)S(1)} %get-tuple-element.25.x_ref, bf16[4,320,128]{2,1,0:T(8,128)(2,1)S(1)} %copy-done, bf16[4,320,128]{2,1,0:T(8,128)(2,1)S(1)} %collective-permute-done.refs_1_, bf16[4,320,128]{2,1,0:T(8,128)(2,1)S(1)} %collective-permute-done.1.refs_2_, ...), custom_call_target="tpu_custom_call" | custom-call | tf_op jit(solution)/shard_map/prepare/pallas_call | solution.py:236
  42.7 0.0 collective-permute-done.7.near_ref
  42.7 0.0 collective-permute-done.8.wide_ref
  42.7 12.4 %first.1 = (bf16[16,336,128]{2,1,0:T(8,128)(2,1)S(1)}, bf16[4,5120,128]{2,1,0:T(8,128)(2,1)S(1)}) custom-call(bf16[2048,5120]{1,0:T(8,128)(2,1)S(1)} %get-tuple-element.25.x_ref, f32[16,16,128]{2,1,0:T(8,128)S(1)} %get-tuple-element.27.squares_ref, f32[2048,256]{1,0:T(8,128)S(1)} %get-tuple-element.31.part_ref, ...), custom_call_target="tpu_custom_call", output_to_operand_aliasing={{1}: (3, {})} | custom-call | tf_op jit(solution)/shard_map/first/pallas_call | solution.py:236
  55.2 22.6 %all_to_all.25.parts_ref = bf16[16,336,128]{2,1,0:T(8,128)(2,1)S(1)} all-to-all(bf16[16,336,128]{2,1,0:T(8,128)(2,1)S(1)} %get-tuple-element.33), channel_id=1, replica_groups=mesh['dp'=16,'mp'=8] {'dp'}, dimensions={0} | all-to-all | bytes 2752512 | tf_op jit(solution)/shard_map/all_to_all | solution.py:290
  77.7 0.5 residual.1
  78.3 19.8 %all_to_all.26 = bf16[16,320,128]{2,1,0:T(8,128)(2,1)S(1)} all-to-all(bf16[16,320,128]{2,1,0:T(8,128)(2,1)S(1)} %get-tuple-element.34), channel_id=1, replica_groups=mesh['dp'=16,'mp'=8] {'dp'}, dimensions={0} | all-to-all | bytes 2621440 | tf_op jit(solution)/shard_map/all_to_all | solution.py:290
  98.1 9.2 %apply.1 = (bf16[16,320,128]{2,1,0:T(8,128)(2,1)S(1)}, f32[2048,128]{1,0:T(8,128)S(1)}) custom-call(bf16[2048,5120]{1,0:T(8,128)(2,1)S(1)} %get-tuple-element.25.x_ref, bf16[5120,128]{1,0:T(8,128)(2,1)S(1)} %bitcast.6), custom_call_target="tpu_custom_call" | custom-call | tf_op jit(solution)/shard_map/apply/pallas_call | solution.py:236
  107.3 18.5 %all_to_all.27.parts_ref = bf16[16,320,128]{2,1,0:T(8,128)(2,1)S(1)} all-to-all(bf16[16,320,128]{2,1,0:T(8,128)(2,1)S(1)} %get-tuple-element.36), channel_id=1, replica_groups=mesh['dp'=16,'mp'=8] {'dp'}, dimensions={0} | all-to-all | bytes 2621440 | tf_op jit(solution)/shard_map/all_to_all | solution.py:290
  125.8 0.3 image.1
  126.1 17.6 %all_to_all.28 = bf16[16,320,128]{2,1,0:T(8,128)(2,1)S(1)} all-to-all(bf16[16,320,128]{2,1,0:T(8,128)(2,1)S(1)} %get-tuple-element.39), channel_id=1, replica_groups=mesh['dp'=16,'mp'=8] {'dp'}, dimensions={0} | all-to-all | bytes 2621440 | tf_op jit(solution)/shard_map/all_to_all | solution.py:290
  143.6 5.9 %last.1 = (f32[320,128]{1,0:T(8,128)S(1)}, f32[8,128]{1,0:T(8,128)S(1)}, f32[16,8,128]{2,1,0:T(8,128)S(1)}) custom-call(bf16[2048,5120]{1,0:T(8,128)(2,1)S(1)} %get-tuple-element.25.x_ref, f32[2048,128]{1,0:T(8,128)S(1)} %get-tuple-element.35.u_ref, bf16[5120,128]{1,0:T(8,128)(2,1)S(1)} %bitcast.7, bf16[5120,128]{1,0:T(8,128)(2,1)S(1)} %bitcast.8, ...), custom_call_target="tpu_custom_call" | custom-call | tf_op jit(solution)/shard_map/last/pallas_call | solution.py:236
  149.5 11.1 %all_to_all.29.parts_ref = f32[16,8,128]{2,1,0:T(8,128)S(1)} all-to-all(f32[16,8,128]{2,1,0:T(8,128)S(1)} %get-tuple-element.41), channel_id=1, replica_groups=mesh['dp'=16,'mp'=8] {'dp'}, dimensions={0} | all-to-all | bytes 131072 | tf_op jit(solution)/shard_map/all_to_all | solution.py:290
  160.6 0.7 merge.1
Async XLA Ops:
  0.0 16.1 %copy-start = (bf16[4,320,128]{2,1,0:T(8,128)(2,1)S(1)}, bf16[4,320,128]{2,1,0:T(8,128)(2,1)}, u32[]{:S(2)}) copy-start(bf16[4,320,128]{2,1,0:T(8,128)(2,1)} %w_ref.1) | copy-start | bytes 983044
  0.0 13.1 %collective-permute-start.2 = (bf16[4,320,128]{2,1,0:T(8,128)(2,1)}, bf16[4,320,128]{2,1,0:T(8,128)(2,1)S(1)}, u32[]{:S(2)}, u32[]{:S(2)}) collective-permute-start(bf16[4,320,128]{2,1,0:T(8,128)(2,1)} %w_ref.1), channel_id=1, source_target_pairs={{0,24},{1,97},{2,26},{3,99},{4,28},{5,101},{6,30},{7,103},{8,0},{9... | collective-permute-start | bytes 983048 | tf_op jit(solution)/shard_map/ppermute | solution.py:278
  4.1 9.0 %collective-permute-start.1 = (bf16[4,320,128]{2,1,0:T(8,128)(2,1)}, bf16[4,320,128]{2,1,0:T(8,128)(2,1)S(1)}, u32[]{:S(2)}, u32[]{:S(2)}) collective-permute-start(bf16[4,320,128]{2,1,0:T(8,128)(2,1)} %w_ref.1), channel_id=1, source_target_pairs={{0,16},{1,65},{2,18},{3,67},{4,20},{5,69},{6,22},{7,71},{8,24},{9,... | collective-permute-start | bytes 983048 | tf_op jit(solution)/shard_map/ppermute | solution.py:278
  4.1 12.0 %collective-permute-start = (bf16[4,320,128]{2,1,0:T(8,128)(2,1)}, bf16[4,320,128]{2,1,0:T(8,128)(2,1)S(1)}, u32[]{:S(2)}, u32[]{:S(2)}) collective-permute-start(bf16[4,320,128]{2,1,0:T(8,128)(2,1)} %w_ref.1), channel_id=1, source_target_pairs={{0,8},{1,33},{2,10},{3,35},{4,12},{5,37},{6,14},{7,39},{8,16},{9,4... | collective-permute-start | bytes 983048 | tf_op jit(solution)/shard_map/ppermute | solution.py:278
  16.2 11.9 %collective-permute-start.3 = (bf16[2,4,320,128]{3,2,1,0:T(8,128)(2,1)S(1)}, bf16[2,4,320,128]{3,2,1,0:T(8,128)(2,1)S(1)}, u32[]{:S(2)}, u32[]{:S(2)}) collective-permute-start(bf16[2,4,320,128]{3,2,1,0:T(8,128)(2,1)S(1)} %pad_maximum_fusion), channel_id=1, source_target_pairs={{0,32},{1,9},{2,34},{3,11},{4,36},{5,13},{6,38},{7,15},{8,40},{9,1... | collective-permute-start | bytes 1966088 | tf_op jit(solution)/shard_map/ppermute | solution.py:278
  17.9 10.7 %collective-permute-start.6 = (bf16[2,4,320,128]{3,2,1,0:T(8,128)(2,1)S(1)}, bf16[2,4,320,128]{3,2,1,0:T(8,128)(2,1)S(1)}, u32[]{:S(2)}, u32[]{:S(2)}) collective-permute-start(bf16[2,4,320,128]{3,2,1,0:T(8,128)(2,1)S(1)} %pad_maximum_fusion.1), channel_id=1, source_target_pairs={{0,96},{1,25},{2,98},{3,27},{4,100},{5,29},{6,102},{7,31},{8,104},... | collective-permute-start | bytes 1966088 | tf_op jit(solution)/shard_map/ppermute | solution.py:278
  19.6 15.9 %collective-permute-start.5 = (bf16[2,4,320,128]{3,2,1,0:T(8,128)(2,1)S(1)}, bf16[2,4,320,128]{3,2,1,0:T(8,128)(2,1)S(1)}, u32[]{:S(2)}, u32[]{:S(2)}) collective-permute-start(bf16[2,4,320,128]{3,2,1,0:T(8,128)(2,1)S(1)} %pad_maximum_fusion), channel_id=1, source_target_pairs={{0,96},{1,25},{2,98},{3,27},{4,100},{5,29},{6,102},{7,31},{8,104},... | collective-permute-start | bytes 1966088 | tf_op jit(solution)/shard_map/ppermute | solution.py:278
  21.4 14.1 %collective-permute-start.4 = (bf16[2,4,320,128]{3,2,1,0:T(8,128)(2,1)S(1)}, bf16[2,4,320,128]{3,2,1,0:T(8,128)(2,1)S(1)}, u32[]{:S(2)}, u32[]{:S(2)}) collective-permute-start(bf16[2,4,320,128]{3,2,1,0:T(8,128)(2,1)S(1)} %pad_maximum_fusion.1), channel_id=1, source_target_pairs={{0,32},{1,9},{2,34},{3,11},{4,36},{5,13},{6,38},{7,15},{8,40},{9,1... | collective-permute-start | bytes 1966088 | tf_op jit(solution)/shard_map/ppermute | solution.py:278
  28.1 14.6 %collective-permute-start.7 = (bf16[2,4,320,128]{3,2,1,0:T(8,128)(2,1)S(1)}, bf16[2,4,320,128]{3,2,1,0:T(8,128)(2,1)S(1)}, u32[]{:S(2)}, u32[]{:S(2)}) collective-permute-start(bf16[2,4,320,128]{3,2,1,0:T(8,128)(2,1)S(1)} %collective-permute-done.3.refs_4_), channel_id=1, source_target_pairs={{0,32},{1,9},{2,34},{3,11},{4,36},{5,13},{6,38},{7,15},{8,40},{9,1... | collective-permute-start | bytes 1966088 | tf_op jit(solution)/shard_map/ppermute | solution.py:278
  28.6 14.1 %collective-permute-start.8 = (bf16[2,4,320,128]{3,2,1,0:T(8,128)(2,1)S(1)}, bf16[2,4,320,128]{3,2,1,0:T(8,128)(2,1)S(1)}, u32[]{:S(2)}, u32[]{:S(2)}) collective-permute-start(bf16[2,4,320,128]{3,2,1,0:T(8,128)(2,1)S(1)} %collective-permute-done.6.refs_7_), channel_id=1, source_target_pairs={{0,96},{1,25},{2,98},{3,27},{4,100},{5,29},{6,102},{7,31},{8,104},... | collective-permute-start | bytes 1966088 | tf_op jit(solution)/shard_map/ppermute | solution.py:278
